TPU v7x, 512 devices: a whole 4x8x8 slice. The times are simulated.
512 devices in a mesh: dp: 32 (over x, y), segment: 2 (over core), mp: 8 (over z).
Axes of the slice: x: 4, y: 8, z: 8, core: 2. Of those that a mesh axis runs over, the one named last changes fastest.
Arguments:
- frames: bfloat16 [2, 8192, 1280], P(None, ('dp', 'mp')), may hold values from -8 to 8
- dec_states: bfloat16 [2, 2048, 1280], P(None, 'dp'), may hold values from -8 to 8
- out_grad: bfloat16 [2, 2048, 1280], P(None, 'dp'), may hold values from -3 to 3
- frame_lengths: int32 [2, 32, 4], P(None, 'dp'), may hold values from 1 to 128, 256 in all within a row
- token_lengths: int32 [2, 32, 4], P(None, 'dp'), may hold values from 1 to 32, 64 in all within a row
- weights: bfloat16 [2, 4, 1024, 1280], P('segment', None, 'mp'), may hold values from -1 to 1
- norm_gains: float32 [3, 1280], replicated, may hold values from 0.25 to 1.75
- norm_biases: float32 [3, 1280], replicated, may hold values from -2 to 2
Outputs:
- gradient: float32 [2, 3, 1024, 1280], P('segment', None, 'mp')
Inputs may be any that keep to these rules, and one draw needn't show every extreme that they name: `frame_lengths`: the 4 utterance lengths of each micro-batch and group sum to 256. `token_lengths`: the 4 token counts of each micro-batch and group sum to 64.
All inputs are finite; a program needn't handle non-finite values.
Results may differ from a plain program's by a relative error of at most 0.04.
Values may be sent and summed in bfloat16 or wider, within the bound.
No kernel may reach another device: no remote copies, remote signals or barrier semaphores. Data moves between devices by JAX's collectives and lax.ppermute only.
A program may use at most 64 MiB of HBM per device.

v0:
```python
import math
import jax
import jax.numpy as jnp
from jax import lax
from jax.sharding import PartitionSpec as P

HS = 64
EPSILON = 1e-05
ROWS_DIMS = (((0,), (0,)), ((), ()))
FEAT_DIMS = (((1,), (1,)), ((), ()))


def layer_norm(values, norm_gain, offset):
    center = values - jnp.mean(values, axis=-1, keepdims=True)
    variance = jnp.mean(center * center, axis=-1, keepdims=True)
    return center * lax.rsqrt(variance + EPSILON) * norm_gain + offset


def norm_backward(grad_out, values, norm_gain):
    center = values - jnp.mean(values, axis=-1, keepdims=True)
    variance = jnp.mean(center * center, axis=-1, keepdims=True)
    inverse = lax.rsqrt(variance + EPSILON)
    normed = center * inverse
    scaled = grad_out * norm_gain
    return inverse * (
        scaled
        - jnp.mean(scaled, axis=-1, keepdims=True)
        - normed * jnp.mean(scaled * normed, axis=-1, keepdims=True)
    )


def utterance_ids(lengths, row_count):
    bounds = jnp.cumsum(lengths, dtype=jnp.int32)
    places = jnp.arange(row_count, dtype=jnp.int32)
    return jnp.sum((places[:, None] >= bounds[None, :]).astype(jnp.int32), axis=1)


def project(row_block, matrix):
    return lax.dot_general(row_block, matrix, FEAT_DIMS, preferred_element_type=jnp.float32).astype(
        jnp.bfloat16
    )


def outer_rows(left_rows, right_rows):
    return lax.dot_general(left_rows, right_rows, ROWS_DIMS, preferred_element_type=jnp.float32)


def split_heads(row_block):
    return row_block.reshape(row_block.shape[0], -1, HS)


def attend(queries, key_rows, value_rows, allowed):
    scaling = 1.0 / math.sqrt(HS)
    scores = (
        jnp.einsum(
            "qhd,khd->hqk",
            split_heads(queries),
            split_heads(key_rows),
            preferred_element_type=jnp.float32,
        )
        * scaling
    )
    scores = jnp.where(allowed[None], scores, -1e30)
    highest = jnp.max(scores, axis=-1, keepdims=True)
    raised = jnp.exp(scores - highest)
    attn_probs = raised / jnp.sum(raised, axis=-1, keepdims=True)
    context = jnp.einsum(
        "hqk,khd->qhd",
        attn_probs.astype(jnp.bfloat16),
        split_heads(value_rows),
        preferred_element_type=jnp.float32,
    )
    return (context.reshape(queries.shape[0], -1).astype(jnp.bfloat16), attn_probs)


def attend_backward(queries, key_rows, value_rows, attn_probs, grad_context):
    scaling = 1.0 / math.sqrt(HS)
    grad_heads = split_heads(grad_context)
    grad_probs = jnp.einsum(
        "qhd,khd->hqk", grad_heads, split_heads(value_rows), preferred_element_type=jnp.float32
    )
    grad_scores = (
        attn_probs * (grad_probs - jnp.sum(grad_probs * attn_probs, axis=-1, keepdims=True))
    ).astype(jnp.bfloat16)
    key_grad = (
        jnp.einsum(
            "hqk,qhd->khd", grad_scores, split_heads(queries), preferred_element_type=jnp.float32
        )
        * scaling
    )
    key_grad = key_grad.reshape(key_rows.shape[0], -1).astype(jnp.bfloat16)
    value_grad = jnp.einsum(
        "hqk,qhd->khd",
        attn_probs.astype(jnp.bfloat16),
        grad_heads,
        preferred_element_type=jnp.float32,
    )
    value_grad = value_grad.reshape(key_rows.shape[0], -1).astype(jnp.bfloat16)
    return (key_grad, value_grad)


def spread(block, axis):
    size = lax.axis_size(axis)
    return lax.all_to_all(jnp.broadcast_to(block[None], (size,) + block.shape), axis, 0, 0)


def share_sum(blocks, axis):
    return jnp.sum(lax.all_to_all(blocks, axis, 0, 0).astype(jnp.float32), axis=0)


def swap(block):
    return lax.ppermute(block, "segment", [(0, 1), (1, 0)])


def to_chunks(block, parts):
    high, wide = (block.shape[0] // 8, block.shape[1] // 128)
    tiles = block.reshape(high, 8, wide, 128).transpose(0, 2, 1, 3).reshape(-1, 8, 128)
    each = -(-tiles.shape[0] // parts)
    tiles = jnp.pad(tiles, ((0, each * parts - tiles.shape[0]), (0, 0), (0, 0)))
    return tiles.reshape(parts, each, 8, 128)


def from_chunks(chunks, rows, cols):
    high, wide = (rows // 8, cols // 128)
    tiles = chunks.reshape(-1, 8, 128)[: high * wide]
    return tiles.reshape(high, wide, 8, 128).transpose(0, 2, 1, 3).reshape(rows, cols)


def shards(
    frames, dec_states, out_grad, frame_lengths, token_lengths, weights, norm_gains, norm_biases
):
    core = lax.axis_index("segment")
    first = core == 0
    own = weights[0]
    shard_rows, features = frames.shape[1:]
    mp = lax.axis_size("mp")
    dp = lax.axis_size("dp")
    head_cols = own.shape[1]
    rows = shard_rows * mp
    half = features // 2

    def mine(array):
        return lax.dynamic_index_in_dim(array, core, 0, keepdims=False)

    inputs = mine(frames)
    tokens = mine(dec_states)
    upstream = mine(out_grad)
    frame_ids = utterance_ids(mine(frame_lengths)[0], rows)
    token_ids = utterance_ids(mine(token_lengths)[0], tokens.shape[0])
    out_sent = lax.ppermute(own[3, :, half:], "segment", [(0, 1)])
    out_part = jnp.where(first, own[3, :, :half], out_sent)
    out_part = lax.all_gather(out_part, "mp", axis=0, tiled=True)
    out_rest = swap(out_part)
    enc_full = spread(inputs, "mp").reshape(rows, features)
    other = swap(own)
    enc = jnp.where(first, own, other)
    dec = jnp.where(first, other, own)
    normed = layer_norm(enc_full.astype(jnp.float32), norm_gains[0], norm_biases[0]).astype(
        jnp.bfloat16
    )
    queries = project(normed, enc[0])
    key_rows = project(normed, enc[1])
    value_rows = project(normed, enc[2])
    context, probs = attend(queries, key_rows, value_rows, frame_ids[:, None] == frame_ids[None, :])
    context_full = spread(context, "mp").transpose(1, 0, 2).reshape(rows, mp * head_cols)
    out_mine = jnp.dot(context_full, out_part, preferred_element_type=jnp.float32)
    out_other = jnp.dot(context_full, out_rest, preferred_element_type=jnp.float32)
    summed = jnp.concatenate(
        [jnp.where(first, out_mine, out_other), jnp.where(first, out_other, out_mine)], axis=1
    )
    states_full = (enc_full.astype(jnp.float32) + summed).astype(jnp.bfloat16)
    states = lax.dynamic_slice_in_dim(states_full, lax.axis_index("mp") * shard_rows, shard_rows, 0)
    state_normed = layer_norm(
        states_full.astype(jnp.float32), norm_gains[2], norm_biases[2]
    ).astype(jnp.bfloat16)
    token_normed = layer_norm(tokens.astype(jnp.float32), norm_gains[1], norm_biases[1]).astype(
        jnp.bfloat16
    )
    dec_queries = project(token_normed, dec[0])
    dec_keys = project(state_normed, dec[1])
    dec_values = project(state_normed, dec[2])
    dec_context, dec_probs = attend(
        dec_queries, dec_keys, dec_values, token_ids[:, None] == frame_ids[None, :]
    )
    grad_context = project(upstream, dec[3])
    dec_key_grad, dec_value_grad = attend_backward(
        dec_queries, dec_keys, dec_values, dec_probs, grad_context
    )
    partial = (
        jnp.dot(dec_key_grad, dec[1], preferred_element_type=jnp.float32)
        + jnp.dot(dec_value_grad, dec[2], preferred_element_type=jnp.float32)
    ).astype(jnp.bfloat16)

    def combine(term):
        left, right = (term[:, :half], term[:, half:])
        sent = swap(jnp.where(first, right, left).astype(jnp.bfloat16))
        return (jnp.where(first, left, right) + sent.astype(jnp.float32)).astype(jnp.bfloat16)

    def reduce_groups(term):
        total = share_sum(to_chunks(term, dp), "dp").astype(jnp.bfloat16)
        return from_chunks(spread(total, "dp"), 3 * head_cols, half)

    dec_term = jnp.concatenate(
        [
            outer_rows(dec_key_grad, state_normed),
            outer_rows(dec_value_grad, state_normed),
            outer_rows(dec_context, upstream),
        ]
    )
    pieces = lax.all_to_all(partial.reshape(mp, shard_rows, features), "mp", 0, 0)
    pieces, dec_part = lax.optimization_barrier((pieces, combine(dec_term)))
    dec_total = lax.psum(dec_part, "dp")
    summed = jnp.sum(pieces.astype(jnp.float32), axis=0)
    grads = norm_backward(summed, states.astype(jnp.float32), norm_gains[2]).astype(jnp.bfloat16)
    grads_full = spread(grads, "mp").reshape(rows, features)
    att_grad = project(grads_full, enc[3])
    enc_key_grad, enc_value_grad = attend_backward(queries, key_rows, value_rows, probs, att_grad)
    enc_term = jnp.concatenate(
        [
            outer_rows(enc_key_grad, normed),
            outer_rows(enc_value_grad, normed),
            outer_rows(context, grads_full),
        ]
    )
    enc_total = reduce_groups(combine(enc_term))
    kept = jnp.where(first, enc_total, dec_total)
    got = swap(jnp.where(first, dec_total, enc_total))
    gradient = jnp.concatenate(
        [jnp.where(first, kept, got), jnp.where(first, got, kept)], axis=1
    ).astype(jnp.float32)
    return gradient.reshape(1, 3, head_cols, features)


def solution(mesh):
    placed = (
        P(None, ("dp", "mp"), None),
        P(None, "dp", None),
        P(None, "dp", None),
        P(None, "dp", None),
        P(None, "dp", None),
        P("segment", None, "mp", None),
        P(),
        P(),
    )
    return jax.shard_map(
        shards,
        mesh=mesh,
        in_specs=placed,
        out_specs=P("segment", None, "mp", None),
        check_vma=False,
    )
```

profile of v0, /device:TPU:1, one launch (start us, length us, event | category | flops | bytes accessed | tf_op | source)
XLA Modules:
  0.0 379.2 jit_solution(9192799755561751875)
XLA Ops:
  8.5 10.9 %all-to-all-start = ((bf16[8,32,1280]{2,1,0:T(8,128)(2,1)}), bf16[8,32,1280]{2,1,0:T(8,128)(2,1)S(1)}, u32[]{:S(2)}, u32[]{:S(2)}) async-start(bf16[8,32,1280]{2,1,0:T(8,128)(2,1)} %broadcast_in_dim.31), calls=%async_computation | async-start | bytes 1310720 | tf_op jit(solution)/shard_map/all_to_all | solution.py:104
  19.4 2.9 collective-permute-start
  27.3 12.8 %all-to-all-done = bf16[8,32,1280]{2,1,0:T(8,128)(2,1)S(1)} async-done(((bf16[8,32,1280]{2,1,0:T(8,128)(2,1)}), bf16[8,32,1280]{2,1,0:T(8,128)(2,1)S(1)}, u32[]{:S(2)}, u32[]{:S(2)}) %all-to-all-start) | async-done | bytes 655392 | tf_op jit(solution)/shard_map/all_to_all | solution.py:104
  41.4 1.5 broadcast_select_fusion.1
  44.4 23.2 %all-gather.2.cloned.1.call-done = bf16[1024,640]{1,0:T(8,128)(2,1)} async-done(((bf16[128,640]{1,0:T(8,128)(2,1)}), bf16[1024,640]{1,0:T(8,128)(2,1)}) %all-gather.2.cloned.1.call-update) | async-done | bytes 1310736 | tf_op jit(solution)/shard_map/all_gather | solution.py:152
  67.6 7.2 %collective-permute-start.2 = (bf16[1024,640]{1,0:T(8,128)(2,1)}, bf16[1024,640]{1,0:T(8,128)(2,1)}, u32[]{:S(2)}, u32[]{:S(2)}) collective-permute-start(bf16[1024,640]{1,0:T(8,128)(2,1)} %all-gather.2.cloned.1.call-done), channel_id=1, source_target_pairs={{0,8},{8,0},{1,9},{9,1},{2,10},{10,2},{3,11},{11,3},{4,12},{12,4},... | collective-permute-start | bytes 3932168 | tf_op jit(solution)/shard_map/ppermute | solution.py:112
  77.4 3.9 %all-to-all-start.1 = ((bf16[8,256,128]{1,2,0:T(8,128)(2,1)}), bf16[8,256,128]{1,2,0:T(8,128)(2,1)S(1)}, u32[]{:S(2)}, u32[]{:S(2)}) async-start(bf16[8,256,128]{1,2,0:T(8,128)(2,1)} %broadcast_in_dim.34), calls=%async_computation.1 | async-start | bytes 1048576 | tf_op jit(solution)/shard_map/all_to_all | solution.py:104
  83.4 1.4 copy.34
  85.7 1.4 copy.35
  87.1 12.2 %all-to-all-done.1 = bf16[8,256,128]{1,2,0:T(8,128)(2,1)S(1)} async-done(((bf16[8,256,128]{1,2,0:T(8,128)(2,1)}), bf16[8,256,128]{1,2,0:T(8,128)(2,1)S(1)}, u32[]{:S(2)}, u32[]{:S(2)}) %all-to-all-start.1) | async-done | bytes 524320 | tf_op jit(solution)/shard_map/all_to_all | solution.py:104
  99.3 1.9 fusion.72
  101.2 1.9 broadcast_select_fusion.7
  107.3 2.4 fusion.25
  111.0 1.3 fusion.17
  114.6 2.2 fusion.2
  116.8 3.5 all-to-all-start.2
  120.3 1.6 pad_maximum_fusion
  122.0 2.4 collective-permute-start.3
  126.9 14.1 %all-to-all-done.2 = bf16[8,32,1280]{2,1,0:T(8,128)(2,1)S(1)} async-done(((bf16[8,32,1280]{2,1,0:T(8,128)(2,1)}), bf16[8,32,1280]{2,1,0:T(8,128)(2,1)S(1)}, u32[]{:S(2)}, u32[]{:S(2)}) %all-to-all-start.2) | async-done | bytes 655392 | tf_op jit(solution)/shard_map/all_to_all | solution.py:210
  141.5 22.3 %all_to_all.30 = bf16[8,32,1280]{2,1,0:T(8,128)(2,1)S(1)} all-to-all(bf16[8,32,1280]{2,1,0:T(8,128)(2,1)S(1)} %broadcast_in_dim.37), channel_id=1, replica_groups=mesh['dp'=32,'segment'=2,'mp'=8] {'mp'}, dimensions={0} | all-to-all | bytes 1310720 | tf_op jit(solution)/shard_map/all_to_all | solution.py:104
  163.8 1.4 convolution_convert_fusion
  165.5 1.5 convolution_convert_fusion.7
  167.3 1.4 fusion.16
  169.5 3.2 collective-permute-start.4
  172.7 1.5 collective-permute-done.4
  174.4 23.2 %all_to_all.31 = bf16[32,8,8,128]{3,2,1,0:T(8,128)(2,1)S(1)} all-to-all(bf16[32,8,8,128]{3,2,1,0:T(8,128)(2,1)S(1)} %bitcast.176), channel_id=1, replica_groups=mesh['dp'=32,'segment'=2,'mp'=8] {'dp'}, dimensions={0} | all-to-all | bytes 1048576 | tf_op jit(solution)/shard_map/all_to_all | solution.py:108
  198.6 8.1 %all-to-all-start.5 = ((bf16[32,8,8,128]{3,2,1,0:T(8,128)(2,1)}), bf16[32,8,8,128]{3,2,1,0:T(8,128)(2,1)S(1)}, u32[]{:S(2)}, u32[]{:S(2)}) async-start(bf16[32,8,8,128]{3,2,1,0:T(8,128)(2,1)} %broadcast_in_dim.42), calls=%async_computation.5 | async-start | bytes 1048576 | tf_op jit(solution)/shard_map/all_to_all | solution.py:104
  207.5 13.3 %all-to-all-done.5 = bf16[32,8,8,128]{3,2,1,0:T(8,128)(2,1)S(1)} async-done(((bf16[32,8,8,128]{3,2,1,0:T(8,128)(2,1)}), bf16[32,8,8,128]{3,2,1,0:T(8,128)(2,1)S(1)}, u32[]{:S(2)}, u32[]{:S(2)}) %all-to-all-start.5) | async-done | bytes 524320 | tf_op jit(solution)/shard_map/all_to_all | solution.py:104
  220.8 140.2 %all-reduce.3.cloned.1.call-done = bf16[384,640]{1,0:T(8,128)(2,1)} async-done(((bf16[384,640]{1,0:T(8,128)(2,1)}), bf16[384,640]{1,0:T(8,128)(2,1)}) %all-reduce.3.cloned.1.call-update) | async-done | bytes 491536 | tf_op jit(solution)/shard_map/psum | solution.py:212
  361.1 8.2 %collective-permute-start.5 = (bf16[384,640]{1,0:T(8,128)(2,1)S(1)}, bf16[384,640]{1,0:T(8,128)(2,1)S(1)}, u32[]{:S(2)}, u32[]{:S(2)}) collective-permute-start(bf16[384,640]{1,0:T(8,128)(2,1)S(1)} %broadcast_select_fusion.4), channel_id=1, source_target_pairs={{0,8},{8,0},{1,9},{9,1},{2,10},{10,2},{3,11},{11,3},{4,12},{12,4},... | collective-permute-start | bytes 1474568 | tf_op jit(solution)/shard_map/ppermute | solution.py:112
  369.3 1.5 collective-permute-done.5
  370.9 1.4 maximum_convert_fusion
  (142 shorter events, 29.2 us)
Async XLA Ops:
  6.5 78.3 %copy-start = (bf16[2,64,1280]{2,1,0:T(8,128)(2,1)S(1)}, bf16[2,64,1280]{2,1,0:T(8,128)(2,1)}, u32[]{:S(2)}) copy-start(bf16[2,64,1280]{2,1,0:T(8,128)(2,1)} %param.10) | copy-start | bytes 983044
  6.5 12.9 %copy-start.4 = (bf16[1,4,128,1280]{3,2,1,0:T(8,128)(2,1)S(1)}, bf16[1,4,128,1280]{3,2,1,0:T(8,128)(2,1)}, u32[]{:S(2)}) copy-start(bf16[1,4,128,1280]{3,2,1,0:T(8,128)(2,1)} %param.13) | copy-start | bytes 3932164
  6.5 17.1 %copy-start.20 = (s32[2,1,4]{2,1,0:T(1,128)S(1)}, s32[2,1,4]{2,1,0:T(1,128)}, u32[]{:S(2)}) copy-start(s32[2,1,4]{2,1,0:T(1,128)} %param.11) | copy-start | bytes 100
  6.5 17.1 %copy-start.21 = (s32[2,1,4]{2,1,0:T(1,128)S(1)}, s32[2,1,4]{2,1,0:T(1,128)}, u32[]{:S(2)}) copy-start(s32[2,1,4]{2,1,0:T(1,128)} %param.12) | copy-start | bytes 100
  6.5 17.4 %copy-start.8 = (bf16[2,64,1280]{2,1,0:T(8,128)(2,1)S(1)}, bf16[2,64,1280]{2,1,0:T(8,128)(2,1)}, u32[]{:S(2)}) copy-start(bf16[2,64,1280]{2,1,0:T(8,128)(2,1)} %param.9) | copy-start | bytes 983044
  7.6 18.3 %copy-start.14 = (f32[3,1280]{1,0:T(4,128)S(1)}, f32[3,1280]{1,0:T(4,128)}, u32[]{:S(2)}) copy-start(f32[3,1280]{1,0:T(4,128)} %param.15) | copy-start | bytes 46084
  7.6 18.3 %copy-start.15 = (f32[3,1280]{1,0:T(4,128)S(1)}, f32[3,1280]{1,0:T(4,128)}, u32[]{:S(2)}) copy-start(f32[3,1280]{1,0:T(4,128)} %param.14) | copy-start | bytes 46084
  8.5 31.6 %all-to-all-start = ((bf16[8,32,1280]{2,1,0:T(8,128)(2,1)}), bf16[8,32,1280]{2,1,0:T(8,128)(2,1)S(1)}, u32[]{:S(2)}, u32[]{:S(2)}) async-start(bf16[8,32,1280]{2,1,0:T(8,128)(2,1)} %broadcast_in_dim.31), calls=%async_computation | async-start | bytes 1310720 | tf_op jit(solution)/shard_map/all_to_all | solution.py:104
  19.3 48.2 %all-gather.2.cloned.1.call-start = ((), (), s32[]{:S(2)}) async-start(), calls=%async_computation.6 | async-start | bytes 1474560 | tf_op jit(solution)/shard_map/all_gather | solution.py:152
  19.4 21.6 %collective-permute-start = (bf16[4,128,1280]{2,1,0:T(8,128)(2,1)S(1)}, bf16[4,128,1280]{2,1,0:T(8,128)(2,1)}, u32[]{:S(2)}, u32[]{:S(2)}) collective-permute-start(bf16[4,128,1280]{2,1,0:T(8,128)(2,1)S(1)} %bitcast.177), channel_id=1, source_target_pairs={{0,8},{8,0},{1,9},{9,1},{2,10},{10,2},{3,11},{11,3},{4,12},{12,4},... | collective-permute-start | bytes 3932168 | tf_op jit(solution)/shard_map/ppermute | solution.py:112
  22.3 4.3 %collective-permute-start.1 = (bf16[128,640]{1,0:T(8,128)(2,1)S(1)}, bf16[128,640]{1,0:T(8,128)(2,1)S(1)}, u32[]{:S(2)}, u32[]{:S(2)}) collective-permute-start(bf16[128,640]{1,0:T(8,128)(2,1)S(1)} %slice_bitcast_fusion.18), channel_id=1, source_target_pairs={{0,8},{1,9},{2,10},{3,11},{4,12},{5,13},{6,14},{7,15},{16,24},{17,... | collective-permute-start | bytes 491528 | tf_op jit(solution)/shard_map/ppermute | solution.py:150
  24.0 1.9 copy-start.18
  25.3 50.7 %copy-start.10 = (pred[256,256]{0,1:T(8,128)(4,1)}, pred[256,256]{0,1:T(8,128)(4,1)S(1)}, u32[]{:S(2)}) copy-start(pred[256,256]{0,1:T(8,128)(4,1)S(1)} %broadcast_compare_fusion) | copy-start | bytes 196612
  42.9 41.9 %copy-start.2 = (bf16[4,128,1280]{2,1,0:T(8,128)(2,1)}, bf16[4,128,1280]{2,1,0:T(8,128)(2,1)S(1)}, u32[]{:S(2)}) copy-start(bf16[4,128,1280]{2,1,0:T(8,128)(2,1)S(1)} %get-tuple-element.22) | copy-start | bytes 3932164
  43.3 32.7 %copy-start.22 = (bf16[256,128]{0,1:T(8,128)(2,1)}, bf16[256,128]{0,1:T(8,128)(2,1)S(1)}, u32[]{:S(2)}) copy-start(bf16[256,128]{0,1:T(8,128)(2,1)S(1)} %convolution_convert_fusion.5) | copy-start | bytes 196612
  44.0 32.5 %copy-start.24 = (bf16[256,128]{0,1:T(8,128)(2,1)}, bf16[256,128]{0,1:T(8,128)(2,1)S(1)}, u32[]{:S(2)}) copy-start(bf16[256,128]{0,1:T(8,128)(2,1)S(1)} %convolution_convert_fusion.6) | copy-start | bytes 196612
  44.3 32.2 %copy-start.26 = (bf16[256,128]{0,1:T(8,128)(2,1)}, bf16[256,128]{0,1:T(8,128)(2,1)S(1)}, u32[]{:S(2)}) copy-start(bf16[256,128]{0,1:T(8,128)(2,1)S(1)} %convolution_convert_fusion.4) | copy-start | bytes 196612
  67.6 31.7 %collective-permute-start.2 = (bf16[1024,640]{1,0:T(8,128)(2,1)}, bf16[1024,640]{1,0:T(8,128)(2,1)}, u32[]{:S(2)}, u32[]{:S(2)}) collective-permute-start(bf16[1024,640]{1,0:T(8,128)(2,1)} %all-gather.2.cloned.1.call-done), channel_id=1, source_target_pairs={{0,8},{8,0},{1,9},{9,1},{2,10},{10,2},{3,11},{11,3},{4,12},{12,4},... | collective-permute-start | bytes 3932168 | tf_op jit(solution)/shard_map/ppermute | solution.py:112
  77.4 21.9 %all-to-all-start.1 = ((bf16[8,256,128]{1,2,0:T(8,128)(2,1)}), bf16[8,256,128]{1,2,0:T(8,128)(2,1)S(1)}, u32[]{:S(2)}, u32[]{:S(2)}) async-start(bf16[8,256,128]{1,2,0:T(8,128)(2,1)} %broadcast_in_dim.34), calls=%async_computation.1 | async-start | bytes 1048576 | tf_op jit(solution)/shard_map/all_to_all | solution.py:104
  104.0 1.7 copy-start.12
  112.4 2.2 copy-start.1
  116.8 24.2 %all-to-all-start.2 = ((bf16[8,32,1280]{2,1,0:T(8,128)(2,1)}), bf16[8,32,1280]{2,1,0:T(8,128)(2,1)S(1)}, u32[]{:S(2)}, u32[]{:S(2)}) async-start(bf16[8,32,1280]{2,1,0:T(8,128)(2,1)} %bitcast.37), calls=%async_computation.2 | async-start | bytes 1310720 | tf_op jit(solution)/shard_map/all_to_all | solution.py:210
  122.0 3.9 %collective-permute-start.3 = (bf16[384,640]{1,0:T(8,128)(2,1)S(1)}, bf16[384,640]{1,0:T(8,128)(2,1)S(1)}, u32[]{:S(2)}, u32[]{:S(2)}) collective-permute-start(bf16[384,640]{1,0:T(8,128)(2,1)S(1)} %select_convert_fusion.1), channel_id=1, source_target_pairs={{0,8},{8,0},{1,9},{9,1},{2,10},{10,2},{3,11},{11,3},{4,12},{12,4},... | collective-permute-start | bytes 1474568 | tf_op jit(solution)/shard_map/ppermute | solution.py:112
  163.8 1.7 copy-start.23
  163.8 1.7 copy-start.25
  163.8 1.7 copy-start.31
  165.4 1.5 copy-start.27
  169.5 4.7 %collective-permute-start.4 = (bf16[384,640]{1,0:T(8,128)(2,1)S(1)}, bf16[384,640]{1,0:T(8,128)(2,1)S(1)}, u32[]{:S(2)}, u32[]{:S(2)}) collective-permute-start(bf16[384,640]{1,0:T(8,128)(2,1)S(1)} %select_convert_fusion), channel_id=1, source_target_pairs={{0,8},{8,0},{1,9},{9,1},{2,10},{10,2},{3,11},{11,3},{4,12},{12,4},... | collective-permute-start | bytes 1474568 | tf_op jit(solution)/shard_map/ppermute | solution.py:112
  198.6 22.2 %all-to-all-start.5 = ((bf16[32,8,8,128]{3,2,1,0:T(8,128)(2,1)}), bf16[32,8,8,128]{3,2,1,0:T(8,128)(2,1)S(1)}, u32[]{:S(2)}, u32[]{:S(2)}) async-start(bf16[32,8,8,128]{3,2,1,0:T(8,128)(2,1)} %broadcast_in_dim.42), calls=%async_computation.5 | async-start | bytes 1048576 | tf_op jit(solution)/shard_map/all_to_all | solution.py:104
  206.7 154.3 %all-reduce.3.cloned.1.call-start = ((), (), s32[]{:S(2)}) async-start(), calls=%async_computation.7 | async-start | bytes 983040 | tf_op jit(solution)/shard_map/psum | solution.py:212
  361.0 9.8 %copy-start.6 = (bf16[384,640]{1,0:T(8,128)(2,1)S(1)}, bf16[384,640]{1,0:T(8,128)(2,1)}, u32[]{:S(2)}) copy-start(bf16[384,640]{1,0:T(8,128)(2,1)} %all-reduce.3.cloned.1.call-done) | copy-start | bytes 1474564
  361.1 9.7 %collective-permute-start.5 = (bf16[384,640]{1,0:T(8,128)(2,1)S(1)}, bf16[384,640]{1,0:T(8,128)(2,1)S(1)}, u32[]{:S(2)}, u32[]{:S(2)}) collective-permute-start(bf16[384,640]{1,0:T(8,128)(2,1)S(1)} %broadcast_select_fusion.4), channel_id=1, source_target_pairs={{0,8},{8,0},{1,9},{9,1},{2,10},{10,2},{3,11},{11,3},{4,12},{12,4},... | collective-permute-start | bytes 1474568 | tf_op jit(solution)/shard_map/ppermute | solution.py:112
  (12 other events, 15.6 us)
Sparse Core Ops, SparseCore 0:
  27.4 40.0 all-gather.1
  210.9 150.0 all-reduce.2
where the time goes:
time: 380 us; the launch traced here: 379 us
  waiting for transfers between devices  220 us (58%)
  starting transfers between devices  51.7 us (14%)
  blocking collectives  45.5 us (12%)
  matrix products  25.7 us (7%)
  between operations  14 us (4%)
  other arithmetic  13.8 us (4%)
  local copies, waits for them, and re-layouts  8.81 us (2%)
    psum x1, waiting for transfers between devices, shards(): dec_total = lax.psum(dec_part, 'dp')  140 us
    all_to_all x3, waiting for transfers between devices, spread(): lax.all_to_all(jnp.broadcast_to(block[None], (size,) + block.shape), axis...  38.3 us
    ppermute x5, starting transfers between devices, swap(): return lax.ppermute(block, 'segment', [(0, 1), (1, 0)])  23.9 us
    all_to_all x1, blocking collectives, share_sum(): lax.all_to_all(blocks, axis, 0, 0).astype(jnp.float32)  23.2 us
    all_gather x1, waiting for transfers between devices, shards(): out_part = lax.all_gather(out_part, 'mp', axis=0, tiled=True)  23.2 us
    all_to_all x3, starting transfers between devices, spread(): lax.all_to_all(jnp.broadcast_to(block[None], (size,) + block.shape), axis...  22.8 us
    all_to_all x1, blocking collectives, spread(): lax.all_to_all(jnp.broadcast_to(block[None], (size,) + block.shape), axis...  22.3 us
    all_to_all x1, waiting for transfers between devices, shards(): lax.all_to_all(partial.reshape(mp, shard_rows, features), 'mp', 0, 0)  14.1 us
  transfers between devices with their start and end apart: 12, of which 9 were waited for; matrix products, arithmetic and copies ran while one was open for 5% of the time, Pallas kernels for 0%

commit v1 on v0

--- a/solution.py
+++ b/solution.py
@@ -209,7 +209,10 @@
     )
     pieces = lax.all_to_all(partial.reshape(mp, shard_rows, features), "mp", 0, 0)
     pieces, dec_part = lax.optimization_barrier((pieces, combine(dec_term)))
-    dec_total = lax.psum(dec_part, "dp")
+    count, dec_total = (lax.axis_size("dp"), dec_part)
+    for far in [1 << k for k in range(count.bit_length() - 1)]:
+        pairs = [(i, i ^ far) for i in range(count)]
+        dec_total = dec_total + lax.ppermute(dec_total, "dp", pairs)
     summed = jnp.sum(pieces.astype(jnp.float32), axis=0)
     grads = norm_backward(summed, states.astype(jnp.float32), norm_gains[2]).astype(jnp.bfloat16)
     grads_full = spread(grads, "mp").reshape(rows, features)

time: 380 us -> 298 us (0.78)
  waiting for transfers between devices: 220 us -> 135 us
  blocking collectives: 45.5 us -> 22.3 us
  starting transfers between devices: 51.7 us -> 74.7 us
    psum x1 -> x0, waiting for transfers between devices: 140 us -> none  [shards(): dec_total = lax.psum(dec_part, 'dp')]
    ppermute x0 -> x5, waiting for transfers between devices: none -> 71.1 us  [shards(): dec_total = dec_total + lax.ppermute(dec_total, 'dp', pairs)]
    all_to_all x1 -> x0, blocking collectives: 23.2 us -> none  [share_sum(): lax.all_to_all(blocks, axis, 0, 0).astype(jnp.float32)]
    ppermute x0 -> x5, starting transfers between devices: none -> 20.1 us  [shards(): dec_total = dec_total + lax.ppermute(dec_total, 'dp', pairs)]
    all_to_all x3, waiting for transfers between devices: 38.3 us -> 24.2 us  [spread(): lax.all_to_all(jnp.broadcast_to(block[None], (size,) + block.shape), axis...]
    all_to_all x0 -> x1, starting transfers between devices: none -> 8.36 us  [share_sum(): lax.all_to_all(blocks, axis, 0, 0).astype(jnp.float32)]
  transfers between devices with their start and end apart: 12 -> 17, of which waited for: 9 -> 11; matrix products, arithmetic and copies ran while one was open for 5% -> 7% of each run, Pallas kernels for 0% -> 0%
where the time goes in v1:
time: 298 us; the launch traced here: 297 us
  waiting for transfers between devices  135 us (45%)
  starting transfers between devices  74.7 us (25%)
  matrix products  26.7 us (9%)
  blocking collectives  22.3 us (7%)
  between operations  14 us (5%)
  other arithmetic  13.2 us (4%)
  local copies, waits for them, and re-layouts  10.8 us (4%)
    ppermute x5, waiting for transfers between devices, shards(): dec_total = dec_total + lax.ppermute(dec_total, 'dp', pairs)  71.1 us
    all_to_all x3, waiting for transfers between devices, spread(): lax.all_to_all(jnp.broadcast_to(block[None], (size,) + block.shape), axis...  24.2 us
    all_gather x1, waiting for transfers between devices, shards(): out_part = lax.all_gather(out_part, 'mp', axis=0, tiled=True)  23.1 us
    all_to_all x1, blocking collectives, spread(): lax.all_to_all(jnp.broadcast_to(block[None], (size,) + block.shape), axis...  22.3 us
    all_to_all x3, starting transfers between devices, spread(): lax.all_to_all(jnp.broadcast_to(block[None], (size,) + block.shape), axis...  20.7 us
    ppermute x5, starting transfers between devices, swap(): return lax.ppermute(block, 'segment', [(0, 1), (1, 0)])  20.6 us
    ppermute x5, starting transfers between devices, shards(): dec_total = dec_total + lax.ppermute(dec_total, 'dp', pairs)  20.1 us
    all_to_all x1, waiting for transfers between devices, shards(): lax.all_to_all(partial.reshape(mp, shard_rows, features), 'mp', 0, 0)  14.9 us
  transfers between devices with their start and end apart: 17, of which 11 were waited for; matrix products, arithmetic and copies ran while one was open for 7% of the time, Pallas kernels for 0%

profile of v1, /device:TPU:1, one launch (start us, length us, event | category | flops | bytes accessed | tf_op | source)
XLA Modules:
  0.0 296.8 jit_solution(8018879356043347106)
XLA Ops:
  8.5 10.9 %all-to-all-start = ((bf16[8,32,1280]{2,1,0:T(8,128)(2,1)}), bf16[8,32,1280]{2,1,0:T(8,128)(2,1)S(1)}, u32[]{:S(2)}, u32[]{:S(2)}) async-start(bf16[8,32,1280]{2,1,0:T(8,128)(2,1)} %broadcast_in_dim.31), calls=%async_computation | async-start | bytes 1310720 | tf_op jit(solution)/shard_map/all_to_all | solution.py:104
  19.4 2.9 collective-permute-start
  27.3 12.9 %all-to-all-done = bf16[8,32,1280]{2,1,0:T(8,128)(2,1)S(1)} async-done(((bf16[8,32,1280]{2,1,0:T(8,128)(2,1)}), bf16[8,32,1280]{2,1,0:T(8,128)(2,1)S(1)}, u32[]{:S(2)}, u32[]{:S(2)}) %all-to-all-start) | async-done | bytes 655392 | tf_op jit(solution)/shard_map/all_to_all | solution.py:104
  41.4 1.5 broadcast_select_fusion
  44.4 23.1 %all-gather.2.cloned.1.call-done = bf16[1024,640]{1,0:T(8,128)(2,1)} async-done(((bf16[128,640]{1,0:T(8,128)(2,1)}), bf16[1024,640]{1,0:T(8,128)(2,1)}) %all-gather.2.cloned.1.call-update) | async-done | bytes 1310736 | tf_op jit(solution)/shard_map/all_gather | solution.py:152
  67.5 7.2 %collective-permute-start.2 = (bf16[1024,640]{1,0:T(8,128)(2,1)}, bf16[1024,640]{1,0:T(8,128)(2,1)}, u32[]{:S(2)}, u32[]{:S(2)}) collective-permute-start(bf16[1024,640]{1,0:T(8,128)(2,1)} %all-gather.2.cloned.1.call-done), channel_id=1, source_target_pairs={{0,8},{8,0},{1,9},{9,1},{2,10},{10,2},{3,11},{11,3},{4,12},{12,4},... | collective-permute-start | bytes 3932168 | tf_op jit(solution)/shard_map/ppermute | solution.py:112
  77.3 3.9 %all-to-all-start.1 = ((bf16[8,256,128]{1,2,0:T(8,128)(2,1)}), bf16[8,256,128]{1,2,0:T(8,128)(2,1)S(1)}, u32[]{:S(2)}, u32[]{:S(2)}) async-start(bf16[8,256,128]{1,2,0:T(8,128)(2,1)} %broadcast_in_dim.34), calls=%async_computation.1 | async-start | bytes 1048576 | tf_op jit(solution)/shard_map/all_to_all | solution.py:104
  84.6 1.8 convolution_convert_fusion.11
  87.9 11.3 %all-to-all-done.1 = bf16[8,256,128]{1,2,0:T(8,128)(2,1)S(1)} async-done(((bf16[8,256,128]{1,2,0:T(8,128)(2,1)}), bf16[8,256,128]{1,2,0:T(8,128)(2,1)S(1)}, u32[]{:S(2)}, u32[]{:S(2)}) %all-to-all-start.1) | async-done | bytes 524320 | tf_op jit(solution)/shard_map/all_to_all | solution.py:104
  99.2 1.9 fusion.72
  101.1 1.9 broadcast_select_fusion.7
  106.2 2.4 fusion.25
  113.9 2.2 fusion.2
  116.1 3.5 %all-to-all-start.2 = ((bf16[8,32,1280]{2,1,0:T(8,128)(2,1)}), bf16[8,32,1280]{2,1,0:T(8,128)(2,1)S(1)}, u32[]{:S(2)}, u32[]{:S(2)}) async-start(bf16[8,32,1280]{2,1,0:T(8,128)(2,1)} %bitcast.37), calls=%async_computation.2 | async-start | bytes 1310720 | tf_op jit(solution)/shard_map/all_to_all | solution.py:210
  121.4 2.4 collective-permute-start.3
  125.4 14.9 %all-to-all-done.2 = bf16[8,32,1280]{2,1,0:T(8,128)(2,1)S(1)} async-done(((bf16[8,32,1280]{2,1,0:T(8,128)(2,1)}), bf16[8,32,1280]{2,1,0:T(8,128)(2,1)S(1)}, u32[]{:S(2)}, u32[]{:S(2)}) %all-to-all-start.2) | async-done | bytes 655392 | tf_op jit(solution)/shard_map/all_to_all | solution.py:210
  140.8 22.3 %all_to_all.30 = bf16[8,32,1280]{2,1,0:T(8,128)(2,1)S(1)} all-to-all(bf16[8,32,1280]{2,1,0:T(8,128)(2,1)S(1)} %broadcast_in_dim.37), channel_id=1, replica_groups=mesh['dp'=32,'segment'=2,'mp'=8] {'mp'}, dimensions={0} | all-to-all | bytes 1310720 | tf_op jit(solution)/shard_map/all_to_all | solution.py:104
  168.3 1.7 fusion.16
  170.5 3.2 %collective-permute-start.4 = (bf16[384,640]{1,0:T(8,128)(2,1)S(1)}, bf16[384,640]{1,0:T(8,128)(2,1)S(1)}, u32[]{:S(2)}, u32[]{:S(2)}) collective-permute-start(bf16[384,640]{1,0:T(8,128)(2,1)S(1)} %select_convert_fusion), channel_id=1, source_target_pairs={{0,8},{8,0},{1,9},{9,1},{2,10},{10,2},{3,11},{11,3},{4,12},{12,4},... | collective-permute-start | bytes 1474568 | tf_op jit(solution)/shard_map/ppermute | solution.py:112
  173.7 3.1 %collective-permute-start.5 = (bf16[384,640]{1,0:T(8,128)(2,1)S(1)}, bf16[384,640]{1,0:T(8,128)(2,1)S(1)}, u32[]{:S(2)}, u32[]{:S(2)}) collective-permute-start(bf16[384,640]{1,0:T(8,128)(2,1)S(1)} %add_convert_fusion.2), channel_id=1, source_target_pairs={{0,16},{16,0},{32,48},{48,32},{64,80},{80,64},{96,112},{112,96},{1... | collective-permute-start | bytes 1474568 | tf_op jit(solution)/shard_map/ppermute | solution.py:215
  177.9 8.4 %all-to-all-start.4 = ((bf16[32,8,8,128]{3,2,1,0:T(8,128)(2,1)}), bf16[32,8,8,128]{3,2,1,0:T(8,128)(2,1)S(1)}, u32[]{:S(2)}, u32[]{:S(2)}) async-start(bf16[32,8,8,128]{3,2,1,0:T(8,128)(2,1)} %bitcast.53), calls=%async_computation.4 | async-start | bytes 1048576 | tf_op jit(solution)/shard_map/all_to_all | solution.py:108
  186.2 2.2 collective-permute-done.5
  188.6 4.0 %collective-permute-start.6 = (bf16[384,640]{1,0:T(8,128)(2,1)S(1)}, bf16[384,640]{1,0:T(8,128)(2,1)S(1)}, u32[]{:S(2)}, u32[]{:S(2)}) collective-permute-start(bf16[384,640]{1,0:T(8,128)(2,1)S(1)} %add.150), channel_id=1, source_target_pairs={{0,32},{16,48},{32,0},{48,16},{64,96},{80,112},{96,64},{112,80},{1... | collective-permute-start | bytes 1474568 | tf_op jit(solution)/shard_map/ppermute | solution.py:215
  192.6 28.4 %collective-permute-done.6 = bf16[384,640]{1,0:T(8,128)(2,1)S(1)} collective-permute-done((bf16[384,640]{1,0:T(8,128)(2,1)S(1)}, bf16[384,640]{1,0:T(8,128)(2,1)S(1)}, u32[]{:S(2)}, u32[]{:S(2)}) %collective-permute-start.6) | collective-permute-done | bytes 491552 | tf_op jit(solution)/shard_map/ppermute | solution.py:215
  221.1 5.4 %collective-permute-start.7 = (bf16[384,640]{1,0:T(8,128)(2,1)S(1)}, bf16[384,640]{1,0:T(8,128)(2,1)S(1)}, u32[]{:S(2)}, u32[]{:S(2)}) collective-permute-start(bf16[384,640]{1,0:T(8,128)(2,1)S(1)} %add.151), channel_id=1, source_target_pairs={{0,64},{16,80},{32,96},{48,112},{64,0},{80,16},{96,32},{112,48},{1... | collective-permute-start | bytes 1474568 | tf_op jit(solution)/shard_map/ppermute | solution.py:215
  227.5 6.0 %all-to-all-start.5 = ((bf16[32,8,8,128]{3,2,1,0:T(8,128)(2,1)}), bf16[32,8,8,128]{3,2,1,0:T(8,128)(2,1)S(1)}, u32[]{:S(2)}, u32[]{:S(2)}) async-start(bf16[32,8,8,128]{3,2,1,0:T(8,128)(2,1)} %broadcast_in_dim.42), calls=%async_computation.5 | async-start | bytes 1048576 | tf_op jit(solution)/shard_map/all_to_all | solution.py:104
  233.5 19.7 %collective-permute-done.7 = bf16[384,640]{1,0:T(8,128)(2,1)S(1)} collective-permute-done((bf16[384,640]{1,0:T(8,128)(2,1)S(1)}, bf16[384,640]{1,0:T(8,128)(2,1)S(1)}, u32[]{:S(2)}, u32[]{:S(2)}) %collective-permute-start.7) | collective-permute-done | bytes 491552 | tf_op jit(solution)/shard_map/ppermute | solution.py:215
  253.4 3.1 %collective-permute-start.8 = (bf16[384,640]{1,0:T(8,128)(2,1)S(1)}, bf16[384,640]{1,0:T(8,128)(2,1)S(1)}, u32[]{:S(2)}, u32[]{:S(2)}) collective-permute-start(bf16[384,640]{1,0:T(8,128)(2,1)S(1)} %add.152), channel_id=1, source_target_pairs={{0,128},{16,144},{32,160},{48,176},{64,192},{80,208},{96,224},{112... | collective-permute-start | bytes 1474568 | tf_op jit(solution)/shard_map/ppermute | solution.py:215
  256.5 11.3 %collective-permute-done.8 = bf16[384,640]{1,0:T(8,128)(2,1)S(1)} collective-permute-done((bf16[384,640]{1,0:T(8,128)(2,1)S(1)}, bf16[384,640]{1,0:T(8,128)(2,1)S(1)}, u32[]{:S(2)}, u32[]{:S(2)}) %collective-permute-start.8) | collective-permute-done | bytes 491552 | tf_op jit(solution)/shard_map/ppermute | solution.py:215
  267.9 4.5 %collective-permute-start.9 = (bf16[384,640]{1,0:T(8,128)(2,1)S(1)}, bf16[384,640]{1,0:T(8,128)(2,1)S(1)}, u32[]{:S(2)}, u32[]{:S(2)}) collective-permute-start(bf16[384,640]{1,0:T(8,128)(2,1)S(1)} %add.153), channel_id=1, source_target_pairs={{0,256},{16,272},{32,288},{48,304},{64,320},{80,336},{96,352},{112... | collective-permute-start | bytes 1474568 | tf_op jit(solution)/shard_map/ppermute | solution.py:215
  272.5 9.5 %collective-permute-done.9 = bf16[384,640]{1,0:T(8,128)(2,1)S(1)} collective-permute-done((bf16[384,640]{1,0:T(8,128)(2,1)S(1)}, bf16[384,640]{1,0:T(8,128)(2,1)S(1)}, u32[]{:S(2)}, u32[]{:S(2)}) %collective-permute-start.9) | collective-permute-done | bytes 491552 | tf_op jit(solution)/shard_map/ppermute | solution.py:215
  282.0 4.9 %collective-permute-start.10 = (bf16[384,640]{1,0:T(8,128)(2,1)S(1)}, bf16[384,640]{1,0:T(8,128)(2,1)S(1)}, u32[]{:S(2)}, u32[]{:S(2)}) collective-permute-start(bf16[384,640]{1,0:T(8,128)(2,1)S(1)} %broadcast_select_fusion.4), channel_id=1, source_target_pairs={{0,8},{8,0},{1,9},{9,1},{2,10},{10,2},{3,11},{11,3},{4,12},{12,4},... | collective-permute-start | bytes 1474568 | tf_op jit(solution)/shard_map/ppermute | solution.py:112
  (142 shorter events, 40.4 us)
Async XLA Ops:
  6.5 75.9 %copy-start = (bf16[2,64,1280]{2,1,0:T(8,128)(2,1)S(1)}, bf16[2,64,1280]{2,1,0:T(8,128)(2,1)}, u32[]{:S(2)}) copy-start(bf16[2,64,1280]{2,1,0:T(8,128)(2,1)} %param.10) | copy-start | bytes 983044
  6.5 12.9 %copy-start.4 = (bf16[1,4,128,1280]{3,2,1,0:T(8,128)(2,1)S(1)}, bf16[1,4,128,1280]{3,2,1,0:T(8,128)(2,1)}, u32[]{:S(2)}) copy-start(bf16[1,4,128,1280]{3,2,1,0:T(8,128)(2,1)} %param.13) | copy-start | bytes 3932164
  6.5 17.1 %copy-start.15 = (s32[2,1,4]{2,1,0:T(1,128)S(1)}, s32[2,1,4]{2,1,0:T(1,128)}, u32[]{:S(2)}) copy-start(s32[2,1,4]{2,1,0:T(1,128)} %param.11) | copy-start | bytes 100
  6.5 17.1 %copy-start.16 = (s32[2,1,4]{2,1,0:T(1,128)S(1)}, s32[2,1,4]{2,1,0:T(1,128)}, u32[]{:S(2)}) copy-start(s32[2,1,4]{2,1,0:T(1,128)} %param.12) | copy-start | bytes 100
  6.5 17.4 %copy-start.7 = (bf16[2,64,1280]{2,1,0:T(8,128)(2,1)S(1)}, bf16[2,64,1280]{2,1,0:T(8,128)(2,1)}, u32[]{:S(2)}) copy-start(bf16[2,64,1280]{2,1,0:T(8,128)(2,1)} %param.9) | copy-start | bytes 983044
  7.6 18.3 %copy-start.12 = (f32[3,1280]{1,0:T(4,128)S(1)}, f32[3,1280]{1,0:T(4,128)}, u32[]{:S(2)}) copy-start(f32[3,1280]{1,0:T(4,128)} %param.15) | copy-start | bytes 46084
  7.6 18.3 %copy-start.13 = (f32[3,1280]{1,0:T(4,128)S(1)}, f32[3,1280]{1,0:T(4,128)}, u32[]{:S(2)}) copy-start(f32[3,1280]{1,0:T(4,128)} %param.14) | copy-start | bytes 46084
  8.5 31.6 %all-to-all-start = ((bf16[8,32,1280]{2,1,0:T(8,128)(2,1)}), bf16[8,32,1280]{2,1,0:T(8,128)(2,1)S(1)}, u32[]{:S(2)}, u32[]{:S(2)}) async-start(bf16[8,32,1280]{2,1,0:T(8,128)(2,1)} %broadcast_in_dim.31), calls=%async_computation | async-start | bytes 1310720 | tf_op jit(solution)/shard_map/all_to_all | solution.py:104
  19.3 48.2 %all-gather.2.cloned.1.call-start = ((), (), s32[]{:S(2)}) async-start(), calls=%async_computation.6 | async-start | bytes 1474560 | tf_op jit(solution)/shard_map/all_gather | solution.py:152
  19.4 21.6 %collective-permute-start = (bf16[4,128,1280]{2,1,0:T(8,128)(2,1)S(1)}, bf16[4,128,1280]{2,1,0:T(8,128)(2,1)}, u32[]{:S(2)}, u32[]{:S(2)}) collective-permute-start(bf16[4,128,1280]{2,1,0:T(8,128)(2,1)S(1)} %bitcast.176), channel_id=1, source_target_pairs={{0,8},{8,0},{1,9},{9,1},{2,10},{10,2},{3,11},{11,3},{4,12},{12,4},... | collective-permute-start | bytes 3932168 | tf_op jit(solution)/shard_map/ppermute | solution.py:112
  22.3 4.2 %collective-permute-start.1 = (bf16[128,640]{1,0:T(8,128)(2,1)S(1)}, bf16[128,640]{1,0:T(8,128)(2,1)S(1)}, u32[]{:S(2)}, u32[]{:S(2)}) collective-permute-start(bf16[128,640]{1,0:T(8,128)(2,1)S(1)} %slice_bitcast_fusion.18), channel_id=1, source_target_pairs={{0,8},{1,9},{2,10},{3,11},{4,12},{5,13},{6,14},{7,15},{16,24},{17,... | collective-permute-start | bytes 491528 | tf_op jit(solution)/shard_map/ppermute | solution.py:150
  24.0 1.8 copy-start.14
  25.3 50.6 %copy-start.8 = (pred[256,256]{0,1:T(8,128)(4,1)}, pred[256,256]{0,1:T(8,128)(4,1)S(1)}, u32[]{:S(2)}) copy-start(pred[256,256]{0,1:T(8,128)(4,1)S(1)} %broadcast_compare_fusion) | copy-start | bytes 196612
  42.9 41.7 %copy-start.2 = (bf16[4,128,1280]{2,1,0:T(8,128)(2,1)}, bf16[4,128,1280]{2,1,0:T(8,128)(2,1)S(1)}, u32[]{:S(2)}) copy-start(bf16[4,128,1280]{2,1,0:T(8,128)(2,1)S(1)} %get-tuple-element.21) | copy-start | bytes 3932164
  43.3 32.6 %copy-start.21 = (bf16[256,128]{0,1:T(8,128)(2,1)}, bf16[256,128]{0,1:T(8,128)(2,1)S(1)}, u32[]{:S(2)}) copy-start(bf16[256,128]{0,1:T(8,128)(2,1)S(1)} %convolution_convert_fusion.4) | copy-start | bytes 196612
  44.0 32.5 %copy-start.17 = (bf16[256,128]{0,1:T(8,128)(2,1)}, bf16[256,128]{0,1:T(8,128)(2,1)S(1)}, u32[]{:S(2)}) copy-start(bf16[256,128]{0,1:T(8,128)(2,1)S(1)} %convolution_convert_fusion.6) | copy-start | bytes 196612
  44.4 32.1 %copy-start.19 = (bf16[256,128]{0,1:T(8,128)(2,1)}, bf16[256,128]{0,1:T(8,128)(2,1)S(1)}, u32[]{:S(2)}) copy-start(bf16[256,128]{0,1:T(8,128)(2,1)S(1)} %convolution_convert_fusion.5) | copy-start | bytes 196612
  67.5 31.7 %collective-permute-start.2 = (bf16[1024,640]{1,0:T(8,128)(2,1)}, bf16[1024,640]{1,0:T(8,128)(2,1)}, u32[]{:S(2)}, u32[]{:S(2)}) collective-permute-start(bf16[1024,640]{1,0:T(8,128)(2,1)} %all-gather.2.cloned.1.call-done), channel_id=1, source_target_pairs={{0,8},{8,0},{1,9},{9,1},{2,10},{10,2},{3,11},{11,3},{4,12},{12,4},... | collective-permute-start | bytes 3932168 | tf_op jit(solution)/shard_map/ppermute | solution.py:112
  77.3 21.9 %all-to-all-start.1 = ((bf16[8,256,128]{1,2,0:T(8,128)(2,1)}), bf16[8,256,128]{1,2,0:T(8,128)(2,1)S(1)}, u32[]{:S(2)}, u32[]{:S(2)}) async-start(bf16[8,256,128]{1,2,0:T(8,128)(2,1)} %broadcast_in_dim.34), calls=%async_computation.1 | async-start | bytes 1048576 | tf_op jit(solution)/shard_map/all_to_all | solution.py:104
  104.0 1.8 copy-start.9
  116.1 24.2 %all-to-all-start.2 = ((bf16[8,32,1280]{2,1,0:T(8,128)(2,1)}), bf16[8,32,1280]{2,1,0:T(8,128)(2,1)S(1)}, u32[]{:S(2)}, u32[]{:S(2)}) async-start(bf16[8,32,1280]{2,1,0:T(8,128)(2,1)} %bitcast.37), calls=%async_computation.2 | async-start | bytes 1310720 | tf_op jit(solution)/shard_map/all_to_all | solution.py:210
  121.4 3.8 %collective-permute-start.3 = (bf16[384,640]{1,0:T(8,128)(2,1)S(1)}, bf16[384,640]{1,0:T(8,128)(2,1)S(1)}, u32[]{:S(2)}, u32[]{:S(2)}) collective-permute-start(bf16[384,640]{1,0:T(8,128)(2,1)S(1)} %select_convert_fusion.1), channel_id=1, source_target_pairs={{0,8},{8,0},{1,9},{9,1},{2,10},{10,2},{3,11},{11,3},{4,12},{12,4},... | collective-permute-start | bytes 1474568 | tf_op jit(solution)/shard_map/ppermute | solution.py:112
  164.7 1.7 copy-start.22
  170.5 6.4 %collective-permute-start.4 = (bf16[384,640]{1,0:T(8,128)(2,1)S(1)}, bf16[384,640]{1,0:T(8,128)(2,1)S(1)}, u32[]{:S(2)}, u32[]{:S(2)}) collective-permute-start(bf16[384,640]{1,0:T(8,128)(2,1)S(1)} %select_convert_fusion), channel_id=1, source_target_pairs={{0,8},{8,0},{1,9},{9,1},{2,10},{10,2},{3,11},{11,3},{4,12},{12,4},... | collective-permute-start | bytes 1474568 | tf_op jit(solution)/shard_map/ppermute | solution.py:112
  173.7 14.7 %collective-permute-start.5 = (bf16[384,640]{1,0:T(8,128)(2,1)S(1)}, bf16[384,640]{1,0:T(8,128)(2,1)S(1)}, u32[]{:S(2)}, u32[]{:S(2)}) collective-permute-start(bf16[384,640]{1,0:T(8,128)(2,1)S(1)} %add_convert_fusion.2), channel_id=1, source_target_pairs={{0,16},{16,0},{32,48},{48,32},{64,80},{80,64},{96,112},{112,96},{1... | collective-permute-start | bytes 1474568 | tf_op jit(solution)/shard_map/ppermute | solution.py:215
  177.9 48.6 %all-to-all-start.4 = ((bf16[32,8,8,128]{3,2,1,0:T(8,128)(2,1)}), bf16[32,8,8,128]{3,2,1,0:T(8,128)(2,1)S(1)}, u32[]{:S(2)}, u32[]{:S(2)}) async-start(bf16[32,8,8,128]{3,2,1,0:T(8,128)(2,1)} %bitcast.53), calls=%async_computation.4 | async-start | bytes 1048576 | tf_op jit(solution)/shard_map/all_to_all | solution.py:108
  188.6 32.4 %collective-permute-start.6 = (bf16[384,640]{1,0:T(8,128)(2,1)S(1)}, bf16[384,640]{1,0:T(8,128)(2,1)S(1)}, u32[]{:S(2)}, u32[]{:S(2)}) collective-permute-start(bf16[384,640]{1,0:T(8,128)(2,1)S(1)} %add.150), channel_id=1, source_target_pairs={{0,32},{16,48},{32,0},{48,16},{64,96},{80,112},{96,64},{112,80},{1... | collective-permute-start | bytes 1474568 | tf_op jit(solution)/shard_map/ppermute | solution.py:215
  221.1 32.1 %collective-permute-start.7 = (bf16[384,640]{1,0:T(8,128)(2,1)S(1)}, bf16[384,640]{1,0:T(8,128)(2,1)S(1)}, u32[]{:S(2)}, u32[]{:S(2)}) collective-permute-start(bf16[384,640]{1,0:T(8,128)(2,1)S(1)} %add.151), channel_id=1, source_target_pairs={{0,64},{16,80},{32,96},{48,112},{64,0},{80,16},{96,32},{112,48},{1... | collective-permute-start | bytes 1474568 | tf_op jit(solution)/shard_map/ppermute | solution.py:215
  227.5 44.9 %all-to-all-start.5 = ((bf16[32,8,8,128]{3,2,1,0:T(8,128)(2,1)}), bf16[32,8,8,128]{3,2,1,0:T(8,128)(2,1)S(1)}, u32[]{:S(2)}, u32[]{:S(2)}) async-start(bf16[32,8,8,128]{3,2,1,0:T(8,128)(2,1)} %broadcast_in_dim.42), calls=%async_computation.5 | async-start | bytes 1048576 | tf_op jit(solution)/shard_map/all_to_all | solution.py:104
  253.4 14.4 %collective-permute-start.8 = (bf16[384,640]{1,0:T(8,128)(2,1)S(1)}, bf16[384,640]{1,0:T(8,128)(2,1)S(1)}, u32[]{:S(2)}, u32[]{:S(2)}) collective-permute-start(bf16[384,640]{1,0:T(8,128)(2,1)S(1)} %add.152), channel_id=1, source_target_pairs={{0,128},{16,144},{32,160},{48,176},{64,192},{80,208},{96,224},{112... | collective-permute-start | bytes 1474568 | tf_op jit(solution)/shard_map/ppermute | solution.py:215
  267.9 14.0 %collective-permute-start.9 = (bf16[384,640]{1,0:T(8,128)(2,1)S(1)}, bf16[384,640]{1,0:T(8,128)(2,1)S(1)}, u32[]{:S(2)}, u32[]{:S(2)}) collective-permute-start(bf16[384,640]{1,0:T(8,128)(2,1)S(1)} %add.153), channel_id=1, source_target_pairs={{0,256},{16,272},{32,288},{48,304},{64,320},{80,336},{96,352},{112... | collective-permute-start | bytes 1474568 | tf_op jit(solution)/shard_map/ppermute | solution.py:215
  282.0 6.4 %collective-permute-start.10 = (bf16[384,640]{1,0:T(8,128)(2,1)S(1)}, bf16[384,640]{1,0:T(8,128)(2,1)S(1)}, u32[]{:S(2)}, u32[]{:S(2)}) collective-permute-start(bf16[384,640]{1,0:T(8,128)(2,1)S(1)} %broadcast_select_fusion.4), channel_id=1, source_target_pairs={{0,8},{8,0},{1,9},{9,1},{2,10},{10,2},{3,11},{11,3},{4,12},{12,4},... | collective-permute-start | bytes 1474568 | tf_op jit(solution)/shard_map/ppermute | solution.py:112
  (11 other events, 15.3 us)
Sparse Core Ops, SparseCore 0:
  27.4 40.0 all-gather.1
